TPU v7x, 32 devices: a whole 2x2x4 slice. The times are simulated.
32 devices in a mesh: dp: 8 (over z, y), chan: 4 (over x, core).
Axes of the slice: x: 2, y: 2, z: 4, core: 2. Of those that a mesh axis runs over, the one named last changes fastest.
Arguments:
- images: bfloat16 [256, 10, 14, 1536], P('dp', None, None, 'chan'), may hold values from -6 to 6
- aspect: int32 [256], P('dp'), may hold values from 0 to 1
- reduce_weight: bfloat16 [1536, 768], P('chan'), may hold values from -400 to 400
- reduce_gain: float32 [768], replicated, may hold values from 0.1 to 1.9
- reduce_bias: float32 [768], replicated, may hold values from -3 to 3
- first_weight: bfloat16 [3, 3, 128, 768], replicated, may hold values from -6 to 6
- first_gain: float32 [768], replicated, may hold values from 0.1 to 1.9
- first_bias: float32 [768], replicated, may hold values from -3 to 3
- second_weight: bfloat16 [3, 3, 128, 768], replicated, may hold values from -6 to 6
- second_gain: float32 [768], replicated, may hold values from 0.1 to 1.9
- second_bias: float32 [768], replicated, may hold values from -3 to 3
- expand_weight: bfloat16 [768, 1536], P('chan'), may hold values from -400 to 400
- expand_gain: float32 [1536], P('chan'), may hold values from 0.1 to 1.9
- expand_bias: float32 [1536], P('chan'), may hold values from -3 to 3
- excite_down: bfloat16 [1536, 768], P('chan'), may hold values from -0.3125 to 0.3125
- excite_down_bias: float32 [768], replicated, may hold values from -3 to 3
- excite_up: bfloat16 [768, 1536], P(None, 'chan'), may hold values from -0.4375 to 0.4375
- excite_up_bias: float32 [1536], P('chan'), may hold values from -3 to 3
- skip_gain: float32 [1], replicated, may hold values from 3 to 6
- out_grad: bfloat16 [256, 10, 14, 1536], P('dp', None, None, 'chan'), may hold values from -6 to 6
Outputs:
- block_out: bfloat16 [256, 10, 14, 1536], P('dp', None, None, 'chan')
- images_grad: float32 [256, 10, 14, 1536], P('dp', None, None, 'chan')
- reduce_weight_grad: float32 [1536, 768], P('chan')
- reduce_gain_grad: float32 [768], replicated
- reduce_bias_grad: float32 [768], replicated
- first_weight_grad: float32 [3, 3, 128, 768], replicated
- first_gain_grad: float32 [768], replicated
- first_bias_grad: float32 [768], replicated
- second_weight_grad: float32 [3, 3, 128, 768], replicated
- second_gain_grad: float32 [768], replicated
- second_bias_grad: float32 [768], replicated
- expand_weight_grad: float32 [768, 1536], P('chan')
- expand_gain_grad: float32 [1536], P('chan')
- expand_bias_grad: float32 [1536], P('chan')
- excite_down_grad: float32 [1536, 768], P('chan')
- excite_down_bias_grad: float32 [768], replicated
- excite_up_grad: float32 [768, 1536], P(None, 'chan')
- excite_up_bias_grad: float32 [1536], P('chan')
- skip_gain_grad: float32 [1], replicated
Inputs may be any that keep to these rules, and one draw needn't show every extreme that they name: `aspect`: 0: the image is 10 rows by 14 columns as stored; 1: it is 14 rows by 10 columns, stored transposed.
All inputs are finite; a program needn't handle non-finite values.
Results may differ from a plain program's by a relative error of at most 0.025.
The roundings to bfloat16 on the way count: a program that leaves them out, or rounds other values in their place, can miss the bound.
Values may be sent and summed in bfloat16 or wider, within the bound.
A program may use at most 256 MiB of HBM per device.

v0:
```python
import jax
import jax.numpy as jnp
from jax import lax
from jax.sharding import PartitionSpec as P

INV_BETA = 1.0 / 1.16619037896906
ALPHA_RES = 0.2
GELU_SCALE = 1.7015
STD_EPSILON = 0.0001
PRECISE = lax.Precision.HIGHEST
NUMBERS = ("NHWC", "HWIO", "NHWC")


def gelu_scaled(value):
    return GELU_SCALE * jax.nn.gelu(value, approximate=True)


def gelu_plain(value):
    return jax.nn.gelu(value, approximate=True)


def backward_of(function, primal, cotangent):
    _, pullback = jax.vjp(function, primal)
    return pullback(cotangent)[0]


def standardize(weight, axes):
    middle = jnp.mean(weight, axis=axes, keepdims=True)
    centered = weight - middle
    spread = jnp.mean(centered * centered, axis=axes, keepdims=True)
    fan_in = 1
    for dimension in axes:
        fan_in = fan_in * weight.shape[dimension]
    return centered * lax.rsqrt(spread * fan_in + STD_EPSILON)


def standardize_group(weight):
    return standardize(weight, (0, 1, 2))


def column_moments(total, squares, fan_in):
    middle = total / fan_in
    spread = squares / fan_in - middle * middle
    return (middle, lax.rsqrt(spread * fan_in + STD_EPSILON))


def standard_grad(summed, centered, rate, column_sum, column_cross, fan_in):
    return rate * (summed - column_sum / fan_in) - rate * rate * rate * centered * column_cross


def group_conv(values, kernel, groups):
    return lax.conv_general_dilated(
        values,
        kernel,
        (1, 1),
        "SAME",
        dimension_numbers=NUMBERS,
        feature_group_count=groups,
        preferred_element_type=jnp.float32,
    )


def group_input_grad(cotangent, kernel, groups):
    taps = kernel.shape[2]
    parted = kernel.reshape(3, 3, taps, groups, taps)
    swapped = jnp.transpose(parted, (0, 1, 4, 3, 2)).reshape(3, 3, taps, groups * taps)[::-1, ::-1]
    return group_conv(cotangent, swapped, groups)


def group_weight_grad(values, cotangent, groups):
    height, width = (values.shape[1], values.shape[2])
    taps = values.shape[3] // groups
    padded = jnp.pad(values, ((0, 0), (1, 1), (1, 1), (0, 0)))
    parted_grad = cotangent.reshape(cotangent.shape[:3] + (groups, taps))
    kernel_rows = []
    for shift_h in range(3):
        row_terms = []
        for shift_w in range(3):
            window = padded[:, shift_h : shift_h + height, shift_w : shift_w + width, :]
            window = window.reshape(window.shape[:3] + (groups, taps))
            product = jnp.einsum(
                "nhwgi,nhwgo->igo", window, parted_grad, preferred_element_type=jnp.float32
            )
            row_terms.append(product.reshape(taps, groups * taps))
        kernel_rows.append(jnp.stack(row_terms))
    return jnp.stack(kernel_rows)


def oriented_conv(values, kernel, aspects, groups):
    plain = group_conv(values, kernel, groups)
    turned = group_conv(values, jnp.transpose(kernel, (1, 0, 2, 3)), groups)
    return jnp.where((aspects == 1)[:, None, None, None], turned, plain)


def oriented_back(values, cotangent, kernel, aspects, groups):
    turned_mask = (aspects == 1)[:, None, None, None]
    nothing = jnp.zeros_like(cotangent)
    grad_plain = jnp.where(turned_mask, nothing, cotangent)
    grad_turned = jnp.where(turned_mask, cotangent, nothing)
    kernel_turned = jnp.transpose(kernel, (1, 0, 2, 3))
    grad_values = group_input_grad(grad_plain, kernel, groups) + group_input_grad(
        grad_turned, kernel_turned, groups
    )
    grad_kernel = group_weight_grad(values, grad_plain, groups)
    grad_kernel = grad_kernel + jnp.transpose(
        group_weight_grad(values, grad_turned, groups), (1, 0, 2, 3)
    )
    return (grad_values, grad_kernel)


def body(
    images,
    aspect,
    reduce_weight,
    reduce_gain,
    reduce_bias,
    first_weight,
    first_gain,
    first_bias,
    second_weight,
    second_gain,
    second_bias,
    expand_weight,
    expand_gain,
    expand_bias,
    excite_down,
    excite_down_bias,
    excite_up,
    excite_up_bias,
    skip_gain,
    out_grad,
):
    parts = lax.axis_size("chan")
    index = lax.axis_index("chan")
    n_images = images.shape[0]
    share = n_images // parts
    groups = first_weight.shape[3] // first_weight.shape[2]
    mid_share = expand_weight.shape[0]
    in_share = reduce_weight.shape[0]
    pixel_count = images.shape[1] * images.shape[2]
    reduce_fan = in_share * parts
    expand_fan = mid_share * parts
    reduce32 = reduce_weight.astype(jnp.float32)
    expand32 = expand_weight.astype(jnp.float32)
    moments = lax.psum(
        (
            jnp.sum(reduce32, axis=0),
            jnp.sum(reduce32 * reduce32, axis=0),
            jnp.sum(expand32, axis=0),
            jnp.sum(expand32 * expand32, axis=0),
        ),
        "chan",
    )
    reduce_mean, reduce_rate = column_moments(moments[0], moments[1], reduce_fan)
    expand_mean, expand_rate = column_moments(moments[2], moments[3], expand_fan)
    reduce_center = reduce32 - reduce_mean
    expand_center = expand32 - expand_mean
    kernel_reduce = (reduce_center * reduce_rate).astype(jnp.bfloat16)
    kernel_expand = (expand_center * expand_rate).astype(jnp.bfloat16)
    kernel_first = standardize_group(first_weight.astype(jnp.float32)).astype(jnp.bfloat16)
    kernel_second = standardize_group(second_weight.astype(jnp.float32)).astype(jnp.bfloat16)
    scaled = (images.astype(jnp.float32) * INV_BETA).astype(jnp.bfloat16)
    aspects = lax.dynamic_slice_in_dim(aspect, index * share, share, 0)
    rows = scaled
    pre_reduce = lax.psum_scatter(
        jnp.einsum("nhwc,cm->nhwm", rows, kernel_reduce, preferred_element_type=jnp.float32),
        "chan",
        scatter_dimension=0,
        tiled=True,
    )
    out_reduce = reduce_gain * pre_reduce + reduce_bias
    act_reduce = gelu_scaled(out_reduce).astype(jnp.bfloat16)
    pre_first = oriented_conv(act_reduce, kernel_first, aspects, groups)
    out_first = first_gain * pre_first + first_bias
    act_first = gelu_scaled(out_first).astype(jnp.bfloat16)
    pre_second = oriented_conv(act_first, kernel_second, aspects, groups)
    out_second = second_gain * pre_second + second_bias
    act_second = gelu_scaled(out_second).astype(jnp.bfloat16)
    act_columns = lax.all_to_all(act_second, "chan", split_axis=3, concat_axis=0, tiled=True)
    partials = jnp.einsum(
        "nhwm,mc->nhwc", act_columns, kernel_expand, preferred_element_type=jnp.float32
    )
    pre_expand = lax.psum_scatter(
        partials.astype(jnp.bfloat16), "chan", scatter_dimension=3, tiled=True
    ).astype(jnp.float32)
    out_expand = expand_gain * pre_expand + expand_bias
    pooled = jnp.mean(out_expand, axis=(1, 2))
    down_partial = jnp.dot(pooled, excite_down.astype(jnp.float32), precision=PRECISE)
    down = lax.psum(down_partial, "chan") + excite_down_bias
    hidden = gelu_plain(down)
    upper = jnp.dot(hidden, excite_up.astype(jnp.float32), precision=PRECISE) + excite_up_bias
    sigma = jax.nn.sigmoid(upper)
    gating = 2.0 * sigma
    branch = out_expand * gating[:, None, None, :]
    branch_scale = ALPHA_RES * skip_gain[0]
    block_out = (images.astype(jnp.float32) + branch_scale * branch).astype(jnp.bfloat16)
    grad_out = out_grad.astype(jnp.float32)
    skip_term = ALPHA_RES * jnp.sum(grad_out * branch)
    grad_branch = branch_scale * grad_out
    grad_gating = jnp.sum(grad_branch * out_expand, axis=(1, 2))
    grad_upper = grad_gating * 2.0 * sigma * (1.0 - sigma)
    excite_up_bias_grad = jnp.sum(grad_upper, axis=0)
    excite_up_grad = jnp.dot(hidden.T, grad_upper, precision=PRECISE)
    hidden_partial = jnp.dot(grad_upper, excite_up.astype(jnp.float32).T, precision=PRECISE)
    grad_hidden = lax.psum(hidden_partial.astype(jnp.bfloat16), "chan").astype(jnp.float32)
    grad_down = backward_of(gelu_plain, down, grad_hidden)
    excite_down_bias_grad = jnp.sum(grad_down, axis=0)
    excite_down_grad = jnp.dot(pooled.T, grad_down, precision=PRECISE)
    grad_pooled = jnp.dot(grad_down, excite_down.astype(jnp.float32).T, precision=PRECISE)
    grad_expand = (
        grad_branch * gating[:, None, None, :] + grad_pooled[:, None, None, :] / pixel_count
    )
    expand_gain_grad = jnp.sum(grad_expand * pre_expand, axis=(0, 1, 2))
    expand_bias_grad = jnp.sum(grad_expand, axis=(0, 1, 2))
    grad_pre_expand = (grad_expand * expand_gain).astype(jnp.bfloat16)
    start_columns = jnp.zeros(act_columns.shape, jnp.float32)
    start_kernel = jnp.zeros((mid_share, expand_weight.shape[1]), jnp.float32)
    piece = lax.all_gather(grad_pre_expand, "chan", axis=3, tiled=True)
    start = jnp.int32(0)
    grad_columns = start_columns
    grad_kernel = start_kernel
    kernel_part = lax.dynamic_slice_in_dim(kernel_expand, start, piece.shape[3], 1)
    grad_columns = grad_columns + jnp.einsum(
        "nhwc,mc->nhwm", piece, kernel_part, preferred_element_type=jnp.float32
    )
    grad_block = jnp.einsum("nhwm,nhwc->mc", act_columns, piece, preferred_element_type=jnp.float32)
    grad_kernel = lax.dynamic_update_slice_in_dim(grad_kernel, grad_block, start, 1)
    grad_columns, expand_rows = (grad_columns, grad_kernel)
    grad_act_second = lax.all_to_all(
        grad_columns.astype(jnp.bfloat16), "chan", split_axis=0, concat_axis=3, tiled=True
    )
    expand_column_sum = jnp.sum(expand_rows, axis=0)
    expand_cross = jnp.sum(expand_rows * expand_center, axis=0)
    expand_full = jnp.zeros((1, 1), jnp.float32)
    grad_second = backward_of(gelu_scaled, out_second, grad_act_second.astype(jnp.float32))
    second_gain_term = jnp.sum(grad_second * pre_second, axis=(0, 1, 2))
    second_bias_term = jnp.sum(grad_second, axis=(0, 1, 2))
    grad_pre_second = (grad_second * second_gain).astype(jnp.bfloat16)
    grad_act_first, grad_kernel_second = oriented_back(
        act_first, grad_pre_second, kernel_second, aspects, groups
    )
    grad_first = backward_of(gelu_scaled, out_first, grad_act_first)
    first_gain_term = jnp.sum(grad_first * pre_first, axis=(0, 1, 2))
    first_bias_term = jnp.sum(grad_first, axis=(0, 1, 2))
    grad_pre_first = (grad_first * first_gain).astype(jnp.bfloat16)
    grad_act_reduce, grad_kernel_first = oriented_back(
        act_reduce, grad_pre_first, kernel_first, aspects, groups
    )
    grad_reduce = backward_of(gelu_scaled, out_reduce, grad_act_reduce)
    reduce_gain_term = jnp.sum(grad_reduce * pre_reduce, axis=(0, 1, 2))
    reduce_bias_term = jnp.sum(grad_reduce, axis=(0, 1, 2))
    grad_pre_reduce = (grad_reduce * reduce_gain).astype(jnp.bfloat16)
    piece = lax.all_gather(grad_pre_reduce, "chan", axis=0, tiled=True)
    rows = scaled
    grad_kernel = jnp.einsum("nhwc,nhwm->cm", rows, piece, preferred_element_type=jnp.float32)
    grad_rows = jnp.einsum(
        "nhwm,cm->nhwc", piece, kernel_reduce, preferred_element_type=jnp.float32
    )
    grad_scaled = grad_rows
    grad_kernel_reduce, grad_scaled = (grad_kernel, grad_scaled)
    images_grad = grad_out + INV_BETA * grad_scaled
    reduce_column_sum = jnp.sum(grad_kernel_reduce, axis=0)
    reduce_cross = jnp.sum(grad_kernel_reduce * reduce_center, axis=0)
    sharded = lax.psum(
        (
            grad_kernel_reduce,
            expand_rows,
            excite_down_grad,
            excite_down_bias_grad,
            excite_up_grad,
            excite_up_bias_grad,
            expand_gain_grad,
            expand_bias_grad,
        ),
        "dp",
    )
    shared = lax.psum(
        (
            grad_kernel_first,
            grad_kernel_second,
            reduce_gain_term,
            reduce_bias_term,
            first_gain_term,
            first_bias_term,
            second_gain_term,
            second_bias_term,
            skip_term,
            reduce_column_sum,
            reduce_cross,
            expand_column_sum,
            expand_cross,
            expand_full,
        ),
        ("dp", "chan"),
    )
    expand_summed = sharded[1]
    reduce_weight_grad = standard_grad(
        sharded[0], reduce_center, reduce_rate, shared[9], shared[10], reduce_fan
    )
    expand_weight_grad = standard_grad(
        expand_summed, expand_center, expand_rate, shared[11], shared[12], expand_fan
    )
    first_weight_grad = backward_of(standardize_group, first_weight.astype(jnp.float32), shared[0])
    second_weight_grad = backward_of(
        standardize_group, second_weight.astype(jnp.float32), shared[1]
    )
    return (
        block_out,
        images_grad,
        reduce_weight_grad,
        shared[2],
        shared[3],
        first_weight_grad,
        shared[4],
        shared[5],
        second_weight_grad,
        shared[6],
        shared[7],
        expand_weight_grad,
        sharded[6],
        sharded[7],
        sharded[2],
        sharded[3],
        sharded[4],
        sharded[5],
        shared[8].reshape(1),
    )


def solution(mesh):
    placed = (
        P("dp", None, None, "chan"),
        P("dp"),
        P("chan", None),
        P(),
        P(),
        P(),
        P(),
        P(),
        P(),
        P(),
        P(),
        P("chan", None),
        P("chan"),
        P("chan"),
        P("chan", None),
        P(),
        P(None, "chan"),
        P("chan"),
        P(),
        P("dp", None, None, "chan"),
    )
    return jax.shard_map(
        body,
        mesh=mesh,
        in_specs=placed,
        out_specs=(
            P("dp", None, None, "chan"),
            P("dp", None, None, "chan"),
            P("chan", None),
            P(),
            P(),
            P(),
            P(),
            P(),
            P(),
            P(),
            P(),
            P("chan", None),
            P("chan"),
            P("chan"),
            P("chan", None),
            P(),
            P(None, "chan"),
            P("chan"),
            P(),
        ),
        check_vma=False,
    )
```

profile of v0, /device:TPU:0, one launch (start us, length us, event | category | flops | bytes accessed | tf_op | source)
XLA Modules:
  0.0 1309.5 jit_solution(16552987430906464153)
XLA Ops:
  9.8 12.8 all-reduce.6
  23.8 10.8 fusion.82
  50.0 92.0 %reduce-scatter.5.cloned.1.call-done = f32[8,10,14,768]{3,0,2,1:T(8,128)} async-done(((f32[32,10,14,768]{3,0,2,1:T(8,128)}), f32[8,10,14,768]{3,0,2,1:T(8,128)}) %reduce-scatter.5.cloned.1.call-update) | async-done | bytes 3440656 | tf_op jit(solution)/shard_map/reduce_scatter | solution.py:165
  145.4 4.2 fusion.106
  149.6 6.6 multiply_convert_fusion.2
  156.3 4.7 fusion.276
  161.1 8.3 fusion.72
  169.4 12.9 copy.282
  182.3 37.4 %reshape.338 = bf16[4,2,107520]{2,1,0:T(2,128)(2,1)} reshape(bf16[768,10,8,14]{3,2,1,0:T(8,128)(2,1)} %bitcast.508) | data formatting | bytes 3440640
  219.7 4.4 all-to-all-start
  224.8 21.1 %all-to-all-done = bf16[4,2,107520]{2,1,0:T(2,128)(2,1)} async-done(((bf16[4,2,107520]{2,1,0:T(2,128)(2,1)}), bf16[4,2,107520]{2,1,0:T(2,128)(2,1)}, u32[]{:S(2)}, u32[]{:S(2)}) %all-to-all-start) | async-done | bytes 1720352 | tf_op jit(solution)/shard_map/all_to_all | solution.py:179
  245.8 42.6 %reshape.339 = bf16[768,10,8,14]{3,2,1,0:T(8,128)(2,1)} reshape(bf16[4,2,107520]{2,1,0:T(2,128)(2,1)} %all-to-all-done) | data formatting | bytes 3440640
  288.4 20.3 %copy.283 = bf16[8,10,14,4,192]{4,0,3,2,1:T(8,128)(2,1)} copy(bf16[8,10,14,4,192]{2,0,1,4,3:T(8,128)(2,1)} %bitcast.510) | data formatting | bytes 3440640 | tf_op jit(solution)/shard_map/all_to_all | solution.py:179
  308.7 8.6 convolution_convert_fusion
  317.3 83.1 %copy.341 = bf16[32,10,14,1536]{0,2,1,3:T(8,128)(2,1)} copy(bf16[32,10,14,1536]{3,0,2,1:T(8,128)(2,1)} %convolution_convert_fusion) | data formatting | bytes 27525120
  400.4 72.3 %reshape.336 = bf16[1536,4480]{1,0:T(8,128)(2,1)} reshape(bf16[1536,10,14,32]{3,2,1,0:T(8,128)(2,1)} %bitcast.507) | data formatting | bytes 27525120
  473.4 106.3 %reduce-scatter.7.cloned.1.call-done = bf16[384,4480]{1,0:T(8,128)(2,1)} async-done(((bf16[1536,4480]{1,0:T(8,128)(2,1)}), bf16[384,4480]{1,0:T(8,128)(2,1)}) %reduce-scatter.7.cloned.1.call-update) | async-done | bytes 3440656
  579.7 18.3 %reshape.337 = bf16[384,10,14,32]{3,2,1,0:T(8,128)(2,1)} reshape(bf16[384,4480]{1,0:T(8,128)(2,1)} %reduce-scatter.7.cloned.1.call-done) | data formatting | bytes 6881280
  598.0 18.6 %copy.342 = bf16[32,10,14,384]{3,0,2,1:T(8,128)(2,1)} copy(bf16[32,10,14,384]{0,2,1,3:T(8,128)(2,1)} %bitcast.509) | data formatting | bytes 6881280
  616.6 4.9 fusion.6
  622.6 31.4 %all-reduce.11.cloned.1.call-done = f32[32,768]{1,0:T(8,128)} async-done(((f32[32,768]{1,0:T(8,128)}), f32[32,768]{1,0:T(8,128)}) %all-reduce.11.cloned.1.call-update) | async-done | bytes 98320 | tf_op jit(solution)/shard_map/psum | solution.py:189
  655.9 10.6 psum.194
  669.2 9.0 fusion.14
  700.5 5.2 copy.293
  708.6 6.7 conv_general_dilated.49
  715.3 6.7 conv_general_dilated.48
  722.6 37.5 %all-reduce.4 = (f32[384]{0:T(512)}, f32[384]{0:T(512)}, f32[768]{0:T(1024)}, f32[384]{0:T(512)}) all-reduce(f32[384]{0:T(512)S(1)} %get-tuple-element.96, f32[384]{0:T(512)S(1)} %get-tuple-element.99, f32[768]{0:T(1024)S(1)} %get-tuple-element.139, f32[384]{0:T(512)S(1)} %get-tuple-element.148), channel_id=1, replica_groups=mesh['dp'=8,'chan'=4] {'dp'}, use_global_device_ids=true, to_apply=%region_47.48 | all-reduce | flops 1920 | bytes 15360 | tf_op jit(solution)/shard_map/psum | solution.py:264
  767.1 8.7 convolution_convert_fusion.1
  778.6 4.7 all-to-all-start.1
  783.6 9.5 fusion.272
  793.1 21.6 %all-to-all-done.1 = bf16[32,10,14,192]{3,2,1,0:T(8,128)(2,1)} async-done(((bf16[32,10,14,192]{3,2,1,0:T(8,128)(2,1)}), bf16[32,10,14,192]{3,2,1,0:T(8,128)(2,1)}, u32[]{:S(2)}, u32[]{:S(2)}) %all-to-all-start.1) | async-done | bytes 1720352 | tf_op jit(solution)/shard_map/all_to_all | solution.py:229
  818.0 3.9 copy.286
  822.0 6.8 mul.791
  828.7 6.5 fusion.54
  860.9 4.2 fusion.267
  865.1 8.1 broadcast_select_fusion
  884.2 4.2 fusion.277
  888.4 7.6 fusion.271
  918.0 9.6 fusion.269
  927.8 18.1 %all-gather.5.cloned.1.call-done = bf16[32,10,14,768]{3,0,2,1:T(8,128)(2,1)} async-done(((bf16[8,10,14,768]{3,0,2,1:T(8,128)(2,1)}), bf16[32,10,14,768]{3,0,2,1:T(8,128)(2,1)}) %all-gather.5.cloned.1.call-update) | async-done | bytes 6881296 | tf_op jit(solution)/shard_map/all_gather | solution.py:253
  945.9 8.0 fusion.273
  957.4 160.8 %all-reduce.13.cloned.1.call-done = (f32[3,3,128,768]{2,3,0,1:T(8,128)}, f32[3,3,128,768]{2,3,0,1:T(8,128)}) async-done(((f32[3,3,128,768]{2,3,0,1:T(8,128)}, f32[3,3,128,768]{2,3,0,1:T(8,128)}), (f32[3,3,128,768]{2,3,0,1:T(8,128)}, f32[3,3,128,768]{2,3,0,1:T(8,128)})) %all-reduce.13.cloned.1.call-update) | async-done | bytes 7077904 | tf_op jit(solution)/shard_map/psum | solution.py:277
  1129.8 5.5 copy.298
  1135.3 3.8 broadcast_add_fusion.1
  1139.1 5.2 copy.297
  1144.3 47.2 %all-reduce.2 = (f32[768]{0:T(1024)S(1)}, f32[768]{0:T(1024)S(1)}, f32[768]{0:T(1024)}, f32[768]{0:T(1024)}, f32[768]{0:T(1024)}, /*index=5*/f32[768]{0:T(1024)}...) all-reduce(f32[768]{0:T(1024)S(1)} %get-tuple-element.109, ...), channel_id=1, replica_groups=mesh['dp'=8,'chan'=4] {'dp','chan'}, use_global_device_ids=true, to_apply=%region_22.23 | all-reduce | flops 9217 | bytes 73736 | tf_op jit(solution)/shard_map/psum | solution.py:277
  1191.6 10.7 convert_add_fusion
  1202.2 93.5 %all-reduce.15.cloned.1.call-done = (f32[384,768]{1,0:T(8,128)}, f32[192,1536]{1,0:T(8,128)}, f32[384,768]{1,0:T(8,128)}, f32[768,384]{1,0:T(8,128)}) async-done(((f32[384,768]{1,0:T(8,128)}, f32[192,1536]{1,0:T(8,128)}, f32[384,768]{1,0:T(8,128)}, f32[768,384]{1,0:T(8,128)}), (f32[384,768]{1,0:T(8,128)}, f32[192,1536]{1,0:T(8,128)}, f32[384,768]{1,0:T(8,128)}, ...) | async-done | bytes 4718608 | tf_op jit(solution)/shard_map/psum | solution.py:264
  (326 shorter events, 147.5 us)
Async XLA Ops:
  7.2 646.8 %copy-start = (bf16[768,384]{1,0:T(8,128)(2,1)S(1)}, bf16[768,384]{1,0:T(8,128)(2,1)}, u32[]{:S(2)}) copy-start(bf16[768,384]{1,0:T(8,128)(2,1)} %param.36) | copy-start | bytes 1769476
  7.2 134.7 %reduce-scatter.5.cloned.1.call-start = ((), (), s32[]{:S(2)}) async-start(), calls=%async_computation.4 | async-start | bytes 17203200 | tf_op jit(solution)/shard_map/reduce_scatter | solution.py:165
  48.6 93.4 %copy-start.87 = (f32[768]{0:T(1024)S(1)}, f32[768]{0:T(1024)}, u32[]{:S(2)}) copy-start(f32[768]{0:T(1024)} %param.24) | copy-start | bytes 9220
  48.6 93.4 %copy-start.89 = (f32[768]{0:T(1024)S(1)}, f32[768]{0:T(1024)}, u32[]{:S(2)}) copy-start(f32[768]{0:T(1024)} %param.23) | copy-start | bytes 9220
  50.0 815.1 %copy-start.91 = (pred[8]{0:T(512)(128)(4,1)}, pred[8]{0:T(512)(128)(4,1)S(1)}, u32[]{:S(2)}) copy-start(pred[8]{0:T(512)(128)(4,1)S(1)} %dynamic-slice_compare_fusion) | copy-start | bytes 28
  50.0 95.4 %copy-start.25 = (bf16[3,3,128,768]{2,3,1,0:T(8,128)(2,1)S(1)}, bf16[3,3,128,768]{2,3,1,0:T(8,128)(2,1)}, u32[]{:S(2)}) copy-start(bf16[3,3,128,768]{2,3,1,0:T(8,128)(2,1)} %copy.279) | copy-start | bytes 5308420
  149.6 6.6 copy-start.7
  156.3 4.8 copy-start.17
  156.3 4.8 copy-start.33
  156.3 4.8 copy-start.81
  156.3 4.8 copy-start.82
  161.0 8.4 copy-start.11
  219.7 26.1 %all-to-all-start = ((bf16[4,2,107520]{2,1,0:T(2,128)(2,1)}), bf16[4,2,107520]{2,1,0:T(2,128)(2,1)}, u32[]{:S(2)}, u32[]{:S(2)}) async-start(bf16[4,2,107520]{2,1,0:T(2,128)(2,1)} %reshape.338), calls=%async_computation.1 | async-start | bytes 3440640 | tf_op jit(solution)/shard_map/all_to_all | solution.py:179
  224.1 355.6 %reduce-scatter.7.cloned.1.call-start = ((), (), s32[]{:S(2)}) async-start(), calls=%async_computation.8 | async-start | bytes 17203200
  224.8 542.3 %copy-start.62 = (f32[1536]{0:T(1024)}, f32[1536]{0:T(1024)S(1)}, u32[]{:S(2)}) copy-start(f32[1536]{0:T(1024)S(1)} %get-tuple-element.151) | copy-start | bytes 18436
  224.8 558.8 %copy-start.60 = (f32[1536]{0:T(1024)}, f32[1536]{0:T(1024)S(1)}, u32[]{:S(2)}) copy-start(f32[1536]{0:T(1024)S(1)} %get-tuple-element.152) | copy-start | bytes 18436
  288.4 20.3 %copy-start.22 = (bf16[192,1536]{1,0:T(8,128)(2,1)S(1)}, bf16[192,1536]{1,0:T(8,128)(2,1)}, u32[]{:S(2)}) copy-start(bf16[192,1536]{1,0:T(8,128)(2,1)} %param.31) | copy-start | bytes 1769476
  472.7 181.3 %all-reduce.11.cloned.1.call-start = ((), (), s32[]{:S(2)}) async-start(), calls=%async_computation.5 | async-start | bytes 196608 | tf_op jit(solution)/shard_map/psum | solution.py:189
  598.0 18.6 %copy-start.85 = (f32[384]{0:T(512)S(1)}, f32[384]{0:T(512)}, u32[]{:S(2)}) copy-start(f32[384]{0:T(512)} %param.33) | copy-start | bytes 4612
  598.0 18.6 %copy-start.86 = (f32[384]{0:T(512)S(1)}, f32[384]{0:T(512)}, u32[]{:S(2)}) copy-start(f32[384]{0:T(512)} %param.32) | copy-start | bytes 4612
  616.6 4.9 copy-start.29
  616.6 37.4 %copy-start.79 = (f32[768]{0:T(1024)S(1)}, f32[768]{0:T(1024)}, u32[]{:S(2)}) copy-start(f32[768]{0:T(1024)} %param.35) | copy-start | bytes 9220
  616.6 37.4 %copy-start.97 = (f32[384]{0:T(512)S(1)}, f32[384]{0:T(512)}, u32[]{:S(2)}) copy-start(f32[384]{0:T(512)} %param.37) | copy-start | bytes 4612
  622.5 144.6 %all-gather.3.cloned.1.call-start = ((), (), s32[]{:S(2)}) async-start(), calls=%async_computation.6 | async-start | bytes 17203200 | tf_op jit(solution)/shard_map/all_gather | solution.py:218
  700.5 5.2 copy-start.21
  715.3 47.0 %copy-start.55 = (f32[32,768]{1,0:T(8,128)S(1)}, f32[32,768]{1,0:T(8,128)}, u32[]{:S(2)}) copy-start(f32[32,768]{1,0:T(8,128)} %all-reduce.11.cloned.1.call-done) | copy-start | bytes 294916
  778.6 5.0 copy-start.8
  778.6 36.1 %all-to-all-start.1 = ((bf16[32,10,14,192]{3,2,1,0:T(8,128)(2,1)}), bf16[32,10,14,192]{3,2,1,0:T(8,128)(2,1)}, u32[]{:S(2)}, u32[]{:S(2)}) async-start(bf16[32,10,14,192]{3,2,1,0:T(8,128)(2,1)} %copy.284), calls=%async_computation.2 | async-start | bytes 5242880 | tf_op jit(solution)/shard_map/all_to_all | solution.py:229
  783.3 162.6 %all-gather.5.cloned.1.call-start = ((), (), s32[]{:S(2)}) async-start(), calls=%async_computation.7 | async-start | bytes 8601600 | tf_op jit(solution)/shard_map/all_gather | solution.py:253
  828.7 6.5 copy-start.99
  865.1 8.1 copy-start.16
  873.2 10.9 copy-start.19
  873.2 15.2 %copy-start.100 = (bf16[8,10,14,6,128]{4,0,3,2,1:T(8,128)(2,1)}, bf16[8,10,14,6,128]{4,0,3,2,1:T(8,128)(2,1)S(1)}, u32[]{:S(2)}) copy-start(bf16[8,10,14,6,128]{4,0,3,2,1:T(8,128)(2,1)S(1)} %get-tuple-element.145) | copy-start | bytes 5160964
  896.0 222.2 %all-reduce.13.cloned.1.call-start = ((), (), s32[]{:S(2)}) async-start(), calls=%async_computation.9 | async-start | bytes 14155776 | tf_op jit(solution)/shard_map/psum | solution.py:277
  917.3 28.6 %copy-start.26 = (bf16[384,768]{1,0:T(8,128)(2,1)S(1)}, bf16[384,768]{1,0:T(8,128)(2,1)}, u32[]{:S(2)}) copy-start(bf16[384,768]{1,0:T(8,128)(2,1)} %param.22) | copy-start | bytes 1769476
  917.3 28.6 %copy-start.71 = (f32[768]{0:T(1024)S(1)}, f32[768]{0:T(1024)}, u32[]{:S(2)}) copy-start(f32[768]{0:T(1024)} %copy-done.70) | copy-start | bytes 9220
  917.3 378.4 %all-reduce.15.cloned.1.call-start = ((), (), s32[]{:S(2)}) async-start(), calls=%async_computation.10 | async-start | bytes 9437184 | tf_op jit(solution)/shard_map/psum | solution.py:264
  953.9 164.3 %copy-start.59 = (f32[768]{0:T(1024)S(1)}, f32[768]{0:T(1024)}, u32[]{:S(2)}) copy-start(f32[768]{0:T(1024)} %copy-done.58) | copy-start | bytes 9220
  954.0 167.6 %copy-start.75 = (f32[768]{0:T(1024)S(1)}, f32[768]{0:T(1024)}, u32[]{:S(2)}) copy-start(f32[768]{0:T(1024)} %copy-done.74) | copy-start | bytes 9220
  1118.3 4.8 copy-start.73
  1139.1 5.2 copy-start.77
  1139.1 5.2 copy-start.78
  1139.1 52.4 %copy-start.69 = (f32[768]{0:T(1024)S(1)}, f32[768]{0:T(1024)}, u32[]{:S(2)}) copy-start(f32[768]{0:T(1024)} %copy-done.68) | copy-start | bytes 9220
  1191.5 104.2 %copy-start.23 = (bf16[192,1536]{1,0:T(8,128)(2,1)S(1)}, bf16[192,1536]{1,0:T(8,128)(2,1)}, u32[]{:S(2)}) copy-start(bf16[192,1536]{1,0:T(8,128)(2,1)} %param.31) | copy-start | bytes 1769476
  1191.5 104.2 %copy-start.61 = (f32[1536]{0:T(1024)S(1)}, f32[1536]{0:T(1024)}, u32[]{:S(2)}) copy-start(f32[1536]{0:T(1024)} %copy-done.60) | copy-start | bytes 18436
  1191.5 104.2 %copy-start.63 = (f32[1536]{0:T(1024)S(1)}, f32[1536]{0:T(1024)}, u32[]{:S(2)}) copy-start(f32[1536]{0:T(1024)} %copy-done.62) | copy-start | bytes 18436
  1191.5 104.2 %copy-start.76 = (f32[1536]{0:T(1024)S(1)}, f32[1536]{0:T(1024)}, u32[]{:S(2)}) copy-start(f32[1536]{0:T(1024)} %get-tuple-element.150) | copy-start | bytes 18436
  1202.2 96.2 %copy-start.80 = (f32[768]{0:T(1024)S(1)}, f32[768]{0:T(1024)}, u32[]{:S(2)}) copy-start(f32[768]{0:T(1024)} %get-tuple-element.153) | copy-start | bytes 9220
  (63 other events, 129.8 us)
Sparse Core Ops, SparseCore 0:
  34.7 107.1 reduce-scatter.4
  472.8 106.8 reduce-scatter.6
  622.7 31.2 all-reduce.10
  678.3 88.6 all-gather.2
  896.1 49.7 all-gather.4
  953.9 164.2 all-reduce.12
  1123.9 171.7 all-reduce.14
where the time goes:
time: 1320 us; the launch traced here: 1310 us
  waiting for transfers between devices  548 us (42%)
  local copies, waits for them, and re-layouts  398 us (30%)
  matrix products  157 us (12%)
  blocking collectives  108 us (8%)
  other arithmetic  71.2 us (5%)
  between operations  16.8 us (1%)
    unnamed x216, local copies, waits for them, and re-layouts  305 us
    psum x1, waiting for transfers between devices, body(): lax.psum((grad_kernel_first, grad_kernel_second, reduce_gain_term, reduce...  161 us
    unnamed x8, waiting for transfers between devices  106 us
    psum x1, waiting for transfers between devices, body(): lax.psum((grad_kernel_reduce, expand_rows, excite_down_grad, excite_down_...  93.5 us
    reduce_scatter x1, waiting for transfers between devices, body(): lax.psum_scatter(jnp.einsum('nhwc,cm->nhwm', rows, kernel_reduce, preferr...  92 us
    conv_general_dilated x8, matrix products, group_conv(): lax.conv_general_dilated(values, kernel, (1, 1), 'SAME', dimension_number...  47.9 us
    psum x1, blocking collectives, body(): lax.psum((grad_kernel_first, grad_kernel_second, reduce_gain_term, reduce...  47.2 us
    dot_general x36, matrix products, group_weight_grad(): jnp.einsum('nhwgi,nhwgo->igo', window, parted_grad, preferred_element_typ...  44.3 us
  transfers between devices with their start and end apart: 9, of which 9 were waited for; matrix products, arithmetic and copies ran while one was open for 11% of the time, Pallas kernels for 0%

commit v1 on v0

--- a/solution.py
+++ b/solution.py
@@ -274,25 +274,24 @@
         ),
         "dp",
     )
-    shared = lax.psum(
-        (
-            grad_kernel_first,
-            grad_kernel_second,
-            reduce_gain_term,
-            reduce_bias_term,
-            first_gain_term,
-            first_bias_term,
-            second_gain_term,
-            second_bias_term,
-            skip_term,
-            reduce_column_sum,
-            reduce_cross,
-            expand_column_sum,
-            expand_cross,
-            expand_full,
-        ),
-        ("dp", "chan"),
-    )
+    shared = (
+        grad_kernel_first,
+        grad_kernel_second,
+        reduce_gain_term,
+        reduce_bias_term,
+        first_gain_term,
+        first_bias_term,
+        second_gain_term,
+        second_bias_term,
+        skip_term,
+        reduce_column_sum,
+        reduce_cross,
+        expand_column_sum,
+        expand_cross,
+        expand_full,
+    )
+    for axis in ("chan", "dp"):
+        shared = lax.psum(shared, axis)
     expand_summed = sharded[1]
     reduce_weight_grad = standard_grad(
         sharded[0], reduce_center, reduce_rate, shared[9], shared[10], reduce_fan

time: 1320 us -> 1510 us (1.14)
  waiting for transfers between devices: 548 us -> 765 us
  blocking collectives: 108 us -> 78.5 us
    psum x1, waiting for transfers between devices: 93.5 us -> 273 us  [body(): lax.psum((grad_kernel_reduce, expand_rows, excite_down_grad, excite_down_...]
    all_gather x1, waiting for transfers between devices: 2.63 us -> 88.9 us  [body(): piece = lax.all_gather(grad_pre_expand, 'chan', axis=3, tiled=True)]
    psum x1, waiting for transfers between devices: 161 us -> 128 us  [body(): shared = lax.psum(shared, axis)]
    psum x2, blocking collectives: 84.7 us -> 54.6 us  [body(): shared = lax.psum(shared, axis)]
    all_to_all x1, waiting for transfers between devices: 21.6 us -> 6.25 us  [body(): lax.all_to_all(grad_columns.astype(jnp.bfloat16), 'chan', split_axis=0, c...]
    unnamed x216 -> x232, local copies, waits for them, and re-layouts: 305 us -> 308 us
  transfers between devices with their start and end apart: 9 -> 9, of which waited for: 9 -> 9; matrix products, arithmetic and copies ran while one was open for 11% -> 8% of each run, Pallas kernels for 0% -> 0%
where the time goes in v1:
time: 1510 us; the launch traced here: 1500 us
  waiting for transfers between devices  765 us (51%)
  local copies, waits for them, and re-layouts  400 us (26%)
  matrix products  158 us (10%)
  blocking collectives  78.5 us (5%)
  other arithmetic  71.1 us (5%)
  between operations  17.1 us (1%)
    unnamed x232, local copies, waits for them, and re-layouts  308 us
    psum x1, waiting for transfers between devices, body(): lax.psum((grad_kernel_reduce, expand_rows, excite_down_grad, excite_down_...  273 us
    psum x1, waiting for transfers between devices, body(): shared = lax.psum(shared, axis)  128 us
    unnamed x8, waiting for transfers between devices  106 us
    reduce_scatter x1, waiting for transfers between devices, body(): lax.psum_scatter(jnp.einsum('nhwc,cm->nhwm', rows, kernel_reduce, preferr...  92 us
    all_gather x1, waiting for transfers between devices, body(): piece = lax.all_gather(grad_pre_expand, 'chan', axis=3, tiled=True)  88.9 us
    psum x2, blocking collectives, body(): shared = lax.psum(shared, axis)  54.6 us
    conv_general_dilated x8, matrix products, group_conv(): lax.conv_general_dilated(values, kernel, (1, 1), 'SAME', dimension_number...  47.6 us
  transfers between devices with their start and end apart: 9, of which 9 were waited for; matrix products, arithmetic and copies ran while one was open for 8% of the time, Pallas kernels for 0%

profile of v1, /device:TPU:0, one launch (start us, length us, event | category | flops | bytes accessed | tf_op | source)
XLA Modules:
  0.0 1499.7 jit_solution(11915344168946995817)
XLA Ops:
  9.8 12.8 all-reduce.5
  23.8 10.8 fusion.82
  49.9 92.0 %reduce-scatter.5.cloned.1.call-done = f32[8,10,14,768]{3,0,2,1:T(8,128)} async-done(((f32[32,10,14,768]{3,0,2,1:T(8,128)}), f32[8,10,14,768]{3,0,2,1:T(8,128)}) %reduce-scatter.5.cloned.1.call-update) | async-done | bytes 3440656 | tf_op jit(solution)/shard_map/reduce_scatter | solution.py:165
  145.4 4.2 fusion.106
  149.7 6.6 multiply_convert_fusion.2
  156.3 4.4 fusion.276
  160.8 8.4 fusion.72
  169.2 12.9 copy.282
  182.1 37.7 %reshape.338 = bf16[4,2,107520]{2,1,0:T(2,128)(2,1)} reshape(bf16[768,10,8,14]{3,2,1,0:T(8,128)(2,1)} %bitcast.508) | data formatting | bytes 3440640
  219.8 4.4 all-to-all-start
  224.8 21.1 %all-to-all-done = bf16[4,2,107520]{2,1,0:T(2,128)(2,1)} async-done(((bf16[4,2,107520]{2,1,0:T(2,128)(2,1)}), bf16[4,2,107520]{2,1,0:T(2,128)(2,1)}, u32[]{:S(2)}, u32[]{:S(2)}) %all-to-all-start) | async-done | bytes 1720352 | tf_op jit(solution)/shard_map/all_to_all | solution.py:179
  245.9 42.5 %reshape.339 = bf16[768,10,8,14]{3,2,1,0:T(8,128)(2,1)} reshape(bf16[4,2,107520]{2,1,0:T(2,128)(2,1)} %all-to-all-done) | data formatting | bytes 3440640
  288.4 20.3 %copy.283 = bf16[8,10,14,4,192]{4,0,3,2,1:T(8,128)(2,1)} copy(bf16[8,10,14,4,192]{2,0,1,4,3:T(8,128)(2,1)} %bitcast.510) | data formatting | bytes 3440640 | tf_op jit(solution)/shard_map/all_to_all | solution.py:179
  308.7 8.5 convolution_convert_fusion
  317.2 83.1 %copy.341 = bf16[32,10,14,1536]{0,2,1,3:T(8,128)(2,1)} copy(bf16[32,10,14,1536]{3,0,2,1:T(8,128)(2,1)} %convolution_convert_fusion) | data formatting | bytes 27525120
  400.3 72.3 %reshape.336 = bf16[1536,4480]{1,0:T(8,128)(2,1)} reshape(bf16[1536,10,14,32]{3,2,1,0:T(8,128)(2,1)} %bitcast.507) | data formatting | bytes 27525120
  473.3 106.3 %reduce-scatter.7.cloned.1.call-done = bf16[384,4480]{1,0:T(8,128)(2,1)} async-done(((bf16[1536,4480]{1,0:T(8,128)(2,1)}), bf16[384,4480]{1,0:T(8,128)(2,1)}) %reduce-scatter.7.cloned.1.call-update) | async-done | bytes 3440656
  579.7 18.2 %reshape.337 = bf16[384,10,14,32]{3,2,1,0:T(8,128)(2,1)} reshape(bf16[384,4480]{1,0:T(8,128)(2,1)} %reduce-scatter.7.cloned.1.call-done) | data formatting | bytes 6881280
  597.9 18.6 %copy.342 = bf16[32,10,14,384]{3,0,2,1:T(8,128)(2,1)} copy(bf16[32,10,14,384]{0,2,1,3:T(8,128)(2,1)} %bitcast.509) | data formatting | bytes 6881280
  616.5 5.5 fusion.6
  623.7 31.4 %all-reduce.11.cloned.1.call-done = f32[32,768]{1,0:T(8,128)} async-done(((f32[32,768]{1,0:T(8,128)}), f32[32,768]{1,0:T(8,128)}) %all-reduce.11.cloned.1.call-update) | async-done | bytes 98320 | tf_op jit(solution)/shard_map/psum | solution.py:189
  660.2 11.1 psum.285
  673.6 9.1 fusion.14
  682.7 88.9 %all-gather.3.cloned.1.call-done = bf16[32,10,14,1536]{3,0,2,1:T(8,128)(2,1)} async-done(((bf16[32,10,14,384]{3,0,2,1:T(8,128)(2,1)}), bf16[32,10,14,1536]{3,0,2,1:T(8,128)(2,1)}) %all-gather.3.cloned.1.call-update) | async-done | bytes 13762576 | tf_op jit(solution)/shard_map/all_gather | solution.py:218
  771.6 8.7 convolution_convert_fusion.1
  783.1 4.6 all-to-all-start.1
  812.8 6.3 all-to-all-done.1
  822.4 3.9 copy.286
  826.3 6.8 mul.791
  833.1 6.3 fusion.54
  865.0 4.2 fusion.267
  869.2 8.0 broadcast_select_fusion
  888.4 4.2 fusion.277
  892.6 7.5 fusion.271
  923.0 8.9 fusion.272
  931.9 18.1 %all-gather.5.cloned.1.call-done = bf16[32,10,14,768]{3,0,2,1:T(8,128)(2,1)} async-done(((bf16[8,10,14,768]{3,0,2,1:T(8,128)(2,1)}), bf16[32,10,14,768]{3,0,2,1:T(8,128)(2,1)}) %all-gather.5.cloned.1.call-update) | async-done | bytes 6881296 | tf_op jit(solution)/shard_map/all_gather | solution.py:253
  950.1 8.0 fusion.273
  958.1 128.1 %all-reduce.15.cloned.1.call-done = (f32[3,3,128,768]{2,3,0,1:T(8,128)}, f32[3,3,128,768]{2,3,0,1:T(8,128)}) async-done(((f32[3,3,128,768]{2,3,0,1:T(8,128)}, f32[3,3,128,768]{2,3,0,1:T(8,128)}), (f32[3,3,128,768]{2,3,0,1:T(8,128)}, f32[3,3,128,768]{2,3,0,1:T(8,128)})) %all-reduce.15.cloned.1.call-update) | async-done | bytes 7077904 | tf_op jit(solution)/shard_map/psum | solution.py:294
  1087.0 5.2 copy.294
  1095.1 7.0 conv_general_dilated.49
  1102.1 6.7 conv_general_dilated.48
  1109.5 9.7 fusion.269
  1122.9 12.1 all-reduce.4
  1135.0 42.5 %all-reduce.2 = (f32[768]{0:T(1024)S(1)}, f32[768]{0:T(1024)S(1)}, f32[768]{0:T(1024)}, f32[768]{0:T(1024)}, f32[768]{0:T(1024)}, /*index=5*/f32[768]{0:T(1024)}...) all-reduce(f32[768]{0:T(1024)S(1)} %get-tuple-element.135, ...), channel_id=1, replica_groups=mesh['dp'=8,'chan'=4] {'dp'}, use_global_device_ids=true, to_apply=%region_24.25 | all-reduce | flops 11137 | bytes 89096 | tf_op jit(solution)/shard_map/psum | solution.py:294
  1177.6 10.7 convert_add_fusion
  1188.3 272.9 %all-reduce.13.cloned.1.call-done = (f32[384,768]{1,0:T(8,128)}, f32[3,3,128,768]{2,3,0,1:T(8,128)}, f32[3,3,128,768]{2,3,0,1:T(8,128)}, f32[192,1536]{1,0:T(8,1...) async-done(((f32[384,768]{1,0:T(8,128)}, f32[3,3,128,768]{2,3,0,1:T(8,128)}, f32[3,3,128,768]{2,3,0,1:T(8,128)}, f32[192,1536]{1,0:T(8,128)}, f32[384,768]{1,0:T(8,128)}, ...) | async-done | bytes 11796496 | tf_op jit(solution)/shard_map/psum | solution.py:264
  1472.7 5.2 copy.298
  1481.8 5.3 copy.297
  (342 shorter events, 150.8 us)
Async XLA Ops:
  7.2 647.9 %copy-start = (bf16[768,384]{1,0:T(8,128)(2,1)S(1)}, bf16[768,384]{1,0:T(8,128)(2,1)}, u32[]{:S(2)}) copy-start(bf16[768,384]{1,0:T(8,128)(2,1)} %param.36) | copy-start | bytes 1769476
  7.2 134.8 %reduce-scatter.5.cloned.1.call-start = ((), (), s32[]{:S(2)}) async-start(), calls=%async_computation.4 | async-start | bytes 17203200 | tf_op jit(solution)/shard_map/reduce_scatter | solution.py:165
  48.5 93.5 %copy-start.94 = (f32[768]{0:T(1024)S(1)}, f32[768]{0:T(1024)}, u32[]{:S(2)}) copy-start(f32[768]{0:T(1024)} %param.24) | copy-start | bytes 9220
  48.5 93.5 %copy-start.96 = (f32[768]{0:T(1024)S(1)}, f32[768]{0:T(1024)}, u32[]{:S(2)}) copy-start(f32[768]{0:T(1024)} %param.23) | copy-start | bytes 9220
  49.9 110.8 %copy-start.98 = (pred[8]{0:T(512)(128)(4,1)}, pred[8]{0:T(512)(128)(4,1)S(1)}, u32[]{:S(2)}) copy-start(pred[8]{0:T(512)(128)(4,1)S(1)} %dynamic-slice_compare_fusion) | copy-start | bytes 28
  49.9 95.5 %copy-start.25 = (bf16[3,3,128,768]{2,3,1,0:T(8,128)(2,1)S(1)}, bf16[3,3,128,768]{2,3,1,0:T(8,128)(2,1)}, u32[]{:S(2)}) copy-start(bf16[3,3,128,768]{2,3,1,0:T(8,128)(2,1)} %copy.279) | copy-start | bytes 5308420
  149.7 6.6 copy-start.7
  156.3 4.5 copy-start.85
  156.3 4.5 copy-start.88
  160.8 8.5 copy-start.11
  219.8 26.1 %all-to-all-start = ((bf16[4,2,107520]{2,1,0:T(2,128)(2,1)}), bf16[4,2,107520]{2,1,0:T(2,128)(2,1)}, u32[]{:S(2)}, u32[]{:S(2)}) async-start(bf16[4,2,107520]{2,1,0:T(2,128)(2,1)} %reshape.338), calls=%async_computation.1 | async-start | bytes 3440640 | tf_op jit(solution)/shard_map/all_to_all | solution.py:179
  224.2 355.5 %reduce-scatter.7.cloned.1.call-start = ((), (), s32[]{:S(2)}) async-start(), calls=%async_computation.8 | async-start | bytes 17203200
  224.8 546.8 %copy-start.66 = (f32[1536]{0:T(1024)}, f32[1536]{0:T(1024)S(1)}, u32[]{:S(2)}) copy-start(f32[1536]{0:T(1024)S(1)} %get-tuple-element.165) | copy-start | bytes 18436
  224.8 546.8 %copy-start.68 = (f32[1536]{0:T(1024)}, f32[1536]{0:T(1024)S(1)}, u32[]{:S(2)}) copy-start(f32[1536]{0:T(1024)S(1)} %get-tuple-element.164) | copy-start | bytes 18436
  288.4 20.3 %copy-start.22 = (bf16[192,1536]{1,0:T(8,128)(2,1)S(1)}, bf16[192,1536]{1,0:T(8,128)(2,1)}, u32[]{:S(2)}) copy-start(bf16[192,1536]{1,0:T(8,128)(2,1)} %param.31) | copy-start | bytes 1769476
  472.6 182.4 %all-reduce.11.cloned.1.call-start = ((), (), s32[]{:S(2)}) async-start(), calls=%async_computation.5 | async-start | bytes 196608 | tf_op jit(solution)/shard_map/psum | solution.py:189
  616.5 6.1 copy-start.29
  623.6 148.0 %all-gather.3.cloned.1.call-start = ((), (), s32[]{:S(2)}) async-start(), calls=%async_computation.6 | async-start | bytes 17203200 | tf_op jit(solution)/shard_map/all_gather | solution.py:218
  783.1 35.9 %all-to-all-start.1 = ((bf16[32,10,14,192]{3,2,1,0:T(8,128)(2,1)}), bf16[32,10,14,192]{3,2,1,0:T(8,128)(2,1)}, u32[]{:S(2)}, u32[]{:S(2)}) async-start(bf16[32,10,14,192]{3,2,1,0:T(8,128)(2,1)} %copy.284), calls=%async_computation.2 | async-start | bytes 5242880 | tf_op jit(solution)/shard_map/all_to_all | solution.py:229
  787.7 162.4 %all-gather.5.cloned.1.call-start = ((), (), s32[]{:S(2)}) async-start(), calls=%async_computation.7 | async-start | bytes 8601600 | tf_op jit(solution)/shard_map/all_gather | solution.py:253
  805.6 5.0 copy-start.38
  805.6 5.0 copy-start.59
  805.6 5.0 copy-start.61
  805.6 5.0 copy-start.83
  826.3 6.8 copy-start.86
  826.3 6.8 copy-start.89
  826.3 6.8 copy-start.99
  833.1 6.3 copy-start.107
  869.2 8.1 copy-start.17
  877.3 11.1 copy-start.20
  877.3 15.3 %copy-start.108 = (bf16[8,10,14,6,128]{4,0,3,2,1:T(8,128)(2,1)}, bf16[8,10,14,6,128]{4,0,3,2,1:T(8,128)(2,1)S(1)}, u32[]{:S(2)}) copy-start(bf16[8,10,14,6,128]{4,0,3,2,1:T(8,128)(2,1)S(1)} %get-tuple-element.158) | copy-start | bytes 5160964
  900.2 186.0 %all-reduce.15.cloned.1.call-start = ((), (), s32[]{:S(2)}) async-start(), calls=%async_computation.10 | async-start | bytes 14155776 | tf_op jit(solution)/shard_map/psum | solution.py:294
  921.2 28.9 %copy-start.26 = (bf16[384,768]{1,0:T(8,128)(2,1)S(1)}, bf16[384,768]{1,0:T(8,128)(2,1)}, u32[]{:S(2)}) copy-start(bf16[384,768]{1,0:T(8,128)(2,1)} %param.22) | copy-start | bytes 1769476
  921.2 28.9 %copy-start.77 = (f32[768]{0:T(1024)S(1)}, f32[768]{0:T(1024)}, u32[]{:S(2)}) copy-start(f32[768]{0:T(1024)} %copy-done.76) | copy-start | bytes 9220
  921.2 540.0 %all-reduce.13.cloned.1.call-start = ((), (), s32[]{:S(2)}) async-start(), calls=%async_computation.9 | async-start | bytes 23592960 | tf_op jit(solution)/shard_map/psum | solution.py:264
  1087.0 5.2 copy-start.12
  1102.1 7.3 copy-start.100
  1119.3 15.7 %copy-start.91 = (f32[768]{0:T(1024)S(1)}, f32[768]{0:T(1024)}, u32[]{:S(2)}) copy-start(f32[768]{0:T(1024)} %get-tuple-element.152) | copy-start | bytes 9220
  1119.3 15.7 %copy-start.92 = (f32[384]{0:T(512)S(1)}, f32[384]{0:T(512)}, u32[]{:S(2)}) copy-start(f32[384]{0:T(512)} %get-tuple-element.96) | copy-start | bytes 4612
  1119.3 15.7 %copy-start.93 = (f32[384]{0:T(512)S(1)}, f32[384]{0:T(512)}, u32[]{:S(2)}) copy-start(f32[384]{0:T(512)} %get-tuple-element.99) | copy-start | bytes 4612
  1119.3 15.7 %copy-start.101 = (f32[384]{0:T(512)S(1)}, f32[384]{0:T(512)}, u32[]{:S(2)}) copy-start(f32[384]{0:T(512)} %get-tuple-element.161) | copy-start | bytes 4612
  1119.3 58.3 %copy-start.75 = (f32[768]{0:T(1024)S(1)}, f32[768]{0:T(1024)}, u32[]{:S(2)}) copy-start(f32[768]{0:T(1024)} %copy-done.74) | copy-start | bytes 9220
  1177.6 283.6 %copy-start.65 = (f32[768]{0:T(1024)S(1)}, f32[768]{0:T(1024)}, u32[]{:S(2)}) copy-start(f32[768]{0:T(1024)} %copy-done.64) | copy-start | bytes 9220
  1177.6 287.0 %copy-start.81 = (f32[768]{0:T(1024)S(1)}, f32[768]{0:T(1024)}, u32[]{:S(2)}) copy-start(f32[768]{0:T(1024)} %copy-done.80) | copy-start | bytes 9220
  1461.2 4.8 copy-start.79
  1481.7 5.3 copy-start.37
  1481.7 5.3 copy-start.69
  1481.7 5.3 copy-start.82
  (71 other events, 147.2 us)
Sparse Core Ops, SparseCore 0:
  34.7 107.1 reduce-scatter.4
  472.8 106.8 reduce-scatter.6
  623.7 31.2 all-reduce.10
  682.8 88.7 all-gather.2
  900.3 49.7 all-gather.4
  953.6 132.5 all-reduce.14
  1093.7 367.4 all-reduce.12
